TPU v7x, 128 devices: a whole 4x4x4 slice. The times are simulated.
128 devices in a mesh: seq: 8 (over x, z_hi), role: 2 (over z_lo), exp: 8 (over y, core).
Axes of the slice: x: 4, y: 4, z: 4 (z_hi: 2, z_lo: 2; z = z_hi * 2 + z_lo), core: 2. Of those that a mesh axis runs over, the one named last changes fastest.
Arguments:
- tokens: bfloat16 [2, 65536, 768], P(None, ('seq', 'role', 'exp')), may hold values from -6 to 6
- expert_ids: int32 [2, 65536, 1], P(None, ('seq', 'role', 'exp')), may hold values from 0 to 127; in each aligned block of 512 rows (0 to 511, 512 to 1023, ..., all dimensions but the last counted through in order) at most 8 rows name the same one
- attn_qkv: bfloat16 [768, 2304], P(('seq', 'role')), may hold values from -0.21875 to 0.21875
- attn_out: bfloat16 [768, 768], P(('seq', 'role')), may hold values from -0.21875 to 0.21875
- norm_attn: float32 [768], replicated, may hold values from 0.1 to 1.9
- norm_ffn: float32 [768], replicated, may hold values from 0.1 to 1.9
- router: bfloat16 [768, 128], replicated, may hold values from -0.43164062 to 0.43164062
- expert_in: bfloat16 [128, 768, 3072], P(('seq', 'role', 'exp')), may hold values from -0.21875 to 0.21875
- expert_out: bfloat16 [128, 3072, 768], P(('seq', 'role', 'exp')), may hold values from -0.109375 to 0.109375
Outputs:
- layer_out: bfloat16 [2, 65536, 768], P(None, ('seq', 'role', 'exp'))
Inputs may be any that keep to these rules, and one draw needn't show every extreme that they name: `expert_ids`: in each micro-batch the 512 tokens of one device name any one expert at most 8 times.
All inputs are finite; a program needn't handle non-finite values.
Results may differ from a plain program's by a relative error of at most 0.0058.
Values may be sent and summed in bfloat16 or wider, within the bound.
No kernel may reach another device: no remote copies, remote signals or barrier semaphores. Data moves between devices by JAX's collectives and lax.ppermute only.
A program may use at most 128 MiB of HBM per device.

v0:
```python
import jax
import jax.numpy as jnp
from jax import lax
from jax.sharding import PartitionSpec as P

HEADS = 12
LEN = 512


def scale_rows(values, gain_vec):
    floats = values.astype(jnp.float32)
    return floats * lax.rsqrt(jnp.mean(floats * floats, -1, keepdims=True) + 1e-06) * gain_vec


def add_columns(source, weight_piece):
    return jnp.dot(source, weight_piece, preferred_element_type=jnp.float32)


def body(
    tokens, expert_ids, attn_qkv, attn_out, norm_attn, norm_ffn, router, expert_in, expert_out
):
    batch_count, row_count, model_width = tokens.shape
    token_count = batch_count * row_count
    head_dim = model_width // HEADS
    flat_tokens = tokens.reshape(token_count, model_width)
    normed = scale_rows(flat_tokens, norm_attn).astype(jnp.bfloat16)
    projected = add_columns(
        normed, lax.all_gather(attn_qkv, ("seq", "role"), axis=0, tiled=True)
    ).astype(jnp.bfloat16)
    heads_split = projected.reshape(token_count // LEN, LEN, 3, HEADS, head_dim)

    def attend(sequence):
        scores = jnp.einsum(
            "qhd,khd->hqk", sequence[:, 0], sequence[:, 1], preferred_element_type=jnp.float32
        ) * head_dim ** (-0.5)
        weights = jnp.exp(scores)
        weights_norm = (weights / jnp.sum(weights, -1, keepdims=True)).astype(jnp.bfloat16)
        return jnp.einsum(
            "hqk,khd->qhd", weights_norm, sequence[:, 2], preferred_element_type=jnp.float32
        ).astype(jnp.bfloat16)

    context = lax.map(attend, heads_split).reshape(token_count, model_width)
    mixed = add_columns(context, lax.all_gather(attn_out, ("seq", "role"), axis=0, tiled=True))
    attended = (flat_tokens.astype(jnp.float32) + mixed).astype(jnp.bfloat16)
    normed_ffn = scale_rows(attended, norm_ffn).astype(jnp.bfloat16)
    experts = lax.axis_size(("seq", "role", "exp"))
    capacity = max(2, 2 * row_count // experts)
    chosen_ids = expert_ids.reshape(token_count)
    logits = jnp.dot(normed_ffn, router, preferred_element_type=jnp.float32)
    picked = chosen_ids[:, None] == lax.broadcasted_iota(jnp.int32, (1, experts), 1)
    gate_value = jax.nn.sigmoid(jnp.sum(jnp.where(picked, logits, 0.0), -1))
    marked = picked.reshape(batch_count, row_count, experts)
    triangle = (
        lax.broadcasted_iota(jnp.int32, (row_count, row_count), 0)
        >= lax.broadcasted_iota(jnp.int32, (row_count, row_count), 1)
    ).astype(jnp.bfloat16)
    running = jnp.einsum(
        "ij,bje->bie", triangle, marked.astype(jnp.bfloat16), preferred_element_type=jnp.float32
    )
    slot_index = jnp.sum(jnp.where(marked, running, 0.0), -1).astype(jnp.int32) - 1
    batch_index = lax.broadcasted_iota(jnp.int32, (batch_count, 1), 0)
    position = (
        chosen_ids.reshape(batch_count, row_count) * (batch_count * capacity)
        + batch_index * capacity
        + slot_index
    ).reshape(token_count)
    slots_total = experts * batch_count * capacity
    outgoing = jnp.zeros((slots_total, model_width), jnp.bfloat16).at[position].set(normed_ffn)
    outgoing = outgoing.reshape(experts, batch_count, capacity, model_width)
    weight_in = expert_in[0]
    weight_out = expert_out[0]
    rows_in = lax.all_to_all(
        outgoing, ("seq", "role", "exp"), split_axis=0, concat_axis=0, tiled=True
    )
    old_shape = rows_in.shape
    hidden = jax.nn.relu(
        jnp.dot(rows_in.reshape(-1, model_width), weight_in, preferred_element_type=jnp.float32)
    ).astype(jnp.bfloat16)
    returned_rows = lax.all_to_all(
        jnp.dot(hidden, weight_out, preferred_element_type=jnp.float32)
        .astype(jnp.bfloat16)
        .reshape(old_shape),
        ("seq", "role", "exp"),
        split_axis=0,
        concat_axis=0,
        tiled=True,
    )
    returned_rows = returned_rows.reshape(slots_total, model_width)
    result = returned_rows[position]
    layer_out = (
        attended.astype(jnp.float32) + gate_value[:, None] * result.astype(jnp.float32)
    ).astype(jnp.bfloat16)
    return layer_out.reshape(batch_count, row_count, model_width)


def solution(mesh):
    in_specs = (
        P(None, ("seq", "role", "exp"), None),
        P(None, ("seq", "role", "exp"), None),
        P(("seq", "role"), None),
        P(("seq", "role"), None),
        P(),
        P(),
        P(),
        P(("seq", "role", "exp"), None, None),
        P(("seq", "role", "exp"), None, None),
    )
    out_specs = P(None, ("seq", "role", "exp"), None)
    return jax.shard_map(body, mesh=mesh, in_specs=in_specs, out_specs=out_specs, check_vma=False)
```

profile of v0, /device:TPU:1, one launch (start us, length us, event | category | flops | bytes accessed | tf_op | source)
XLA Modules:
  0.0 254.4 jit_solution(380767495640874659)
XLA Ops:
  6.5 0.7 all-gather.3.cloned.1.call-update
  7.3 0.0 all-gather.5.cloned.1.call-start
  7.3 0.7 all-gather.5.cloned.1.call-update
  8.0 0.7 copy.23
  8.7 0.7 broadcast_multiply_fusion
  9.4 1.8 fusion.20
  11.2 0.4 fusion.28
  11.6 0.1 broadcast_bitcast_fusion
  11.7 1.6 fusion.22
  13.3 48.2 %all-gather.3.cloned.1.call-done = bf16[768,2304]{1,0:T(8,128)(2,1)} async-done(((bf16[48,2304]{1,0:T(8,128)(2,1)}), bf16[768,2304]{1,0:T(8,128)(2,1)}) %all-gather.3.cloned.1.call-update) | async-done | bytes 3538960 | tf_op jit(solution)/shard_map/all_gather | solution.py:28
  61.5 8.4 %convolution_convert_fusion = bf16[1024,2304]{1,0:T(8,128)(2,1)} fusion(bf16[1024,768]{1,0:T(8,128)(2,1)} %fusion.22, bf16[768,2304]{1,0:T(8,128)(2,1)} %all-gather.3.cloned.1.call-done), kind=kOutput, calls=%fused_computation.16 | convolution fusion | flops 3626237952 | bytes 9830400 | tf_op jit(solution)/shard_map/dot_general | solution.py:16
  69.9 6.7 %copy.13 = bf16[1024,2304]{0,1:T(8,128)(2,1)} copy(bf16[1024,2304]{1,0:T(8,128)(2,1)} %convolution_convert_fusion) | data formatting | bytes 9437184 | tf_op jit(solution)/shard_map/convert_element_type | solution.py:29
  76.6 8.8 %reshape.127 = bf16[2,512,3,12,64]{1,0,4,3,2:T(2,128)(2,1)} reshape(bf16[1024,2304]{0,1:T(8,128)(2,1)} %copy.13) | data formatting | bytes 9437184 | tf_op jit(solution)/shard_map/reshape | solution.py:30
  85.5 5.5 %copy.14 = bf16[2,512,3,12,64]{1,4,3,2,0:T(8,128)(2,1)} copy(bf16[2,512,3,12,64]{1,0,4,3,2:T(2,128)(2,1)} %reshape.127) | data formatting | bytes 9437184 | tf_op jit(solution)/shard_map/while | solution.py:42
  91.0 13.4 %while.10 = (s32[]{:T(128)}, bf16[2,512,12,64]{1,3,2,0:T(8,128)(2,1)S(1)}, bf16[2,512,3,12,64]{1,4,3,2,0:T(8,128)(2,1)}, s32[]{:T(128)}) while((s32[]{:T(128)}, bf16[2,512,12,64]{1,3,2,0:T(8,128)(2,1)S(1)}, bf16[2,512,3,12,64]{1,4,3,2,0:T(8,128)(2,1)}, s32[]{:T(128)}) %tuple.24), condition=%wide.region_3.4_spmd, body=%wide.region_1.3_spmd.sunk | while | flops 821422080 | bytes 33087548 | solution.py:42
  91.0 1.9 dynamic-slice_bitcast_fusion.2
  92.9 2.3 fusion.43
  95.2 2.4 fusion.44
  97.7 1.9 dynamic-slice_bitcast_fusion.2
  99.6 2.3 fusion.43
  102.0 2.4 fusion.44
  104.4 1.6 copy.15
  106.0 0.4 copy.19
  106.5 4.0 %fusion.16 = (f32[1024]{0:T(1024)S(1)}, bf16[1024,768]{1,0:T(8,128)(2,1)}) fusion(bf16[1024,768]{0,1:T(8,128)(2,1)S(1)} %bitcast.102, bf16[768,768]{1,0:T(8,128)(2,1)} %all-gather.5.cloned.1.call-done, bf16[2,512,768]{2,1,0:T(8,128)(2,1)S(1)} %copy-done.1), kind=kOutput, calls=%fused_computation.24 | convolution fusion | flops 1212677120 | bytes 5902336 | tf_op jit(solution)/shard_map/dot_general | solution.py:16
  110.5 7.2 %scatter_custom_fusion = bf16[2048,768]{1,0:T(8,128)(2,1)S(1)} fusion(s32[1024]{0:T(1024)S(1)} %bitcast.105, bf16[]{:T(256)} %constant.7.clone.1, bf16[1024,768]{1,0:T(8,128)(2,1)} %get-tuple-element.38, f32[768]{0:T(1024)S(1)} %copy-done.4, f32[1024]{0:T(1024)S(1)} %add_rsqrt_fusion), kind=kCustom, calls=%fused_computation.35 | custom fusion | flops 3145728 | bytes 4726786 | tf_op jit(solution)/shard_map/scatter | solution.py:68
  117.7 49.2 %all_to_all.10 = bf16[128,2,8,768]{3,2,1,0:T(8,128)(2,1)} all-to-all(bf16[128,2,8,768]{3,2,1,0:T(8,128)(2,1)S(1)} %bitcast.98), channel_id=1, replica_groups=mesh['seq'=8,'role'=2,'exp'=8] {'seq','role','exp'}, dimensions={0} | all-to-all | bytes 6291456 | tf_op jit(solution)/shard_map/all_to_all | solution.py:72
  166.9 25.4 %fusion.11 = bf16[2048,768]{1,0:T(8,128)(2,1)} fusion(bf16[1,3072,768]{2,1,0:T(8,128)(2,1)} %param.19, bf16[2048,768]{1,0:T(8,128)(2,1)} %bitcast.101, bf16[1,768,3072]{2,1,0:T(8,128)(2,1)} %param.18), kind=kOutput, calls=%fused_computation.23 | convolution fusion | flops 19341508608 | bytes 15728640 | tf_op jit(solution)/shard_map/dot_general | solution.py:80
  192.3 4.8 %all-to-all-start.1 = ((bf16[128,2,8,768]{3,2,1,0:T(8,128)(2,1)}), bf16[128,2,8,768]{3,2,1,0:T(8,128)(2,1)S(1)}, u32[]{:S(2)}, u32[]{:S(2)}) async-start(bf16[128,2,8,768]{3,2,1,0:T(8,128)(2,1)} %bitcast.100), calls=%async_computation.1 | async-start | bytes 6291456 | tf_op jit(solution)/shard_map/all_to_all | solution.py:79
  197.1 2.2 fusion.27
  199.3 39.5 %all-to-all-done.1 = bf16[128,2,8,768]{3,2,1,0:T(8,128)(2,1)S(1)} async-done(((bf16[128,2,8,768]{3,2,1,0:T(8,128)(2,1)}), bf16[128,2,8,768]{3,2,1,0:T(8,128)(2,1)S(1)}, u32[]{:S(2)}, u32[]{:S(2)}) %all-to-all-start.1) | async-done | bytes 3145760 | tf_op jit(solution)/shard_map/all_to_all | solution.py:79
  238.8 5.2 %gather_fusion = bf16[1024,768]{1,0:T(8,128)(2,1)} fusion(bf16[2048,768]{1,0:T(8,128)(2,1)S(1)} %bitcast.97, s32[1024]{0:T(1024)S(1)} %broadcast_clamp_fusion), kind=kCustom, calls=%fused_computation | custom fusion | bytes 3149824 | tf_op jit(solution)/shard_map/gather | solution.py:89
  244.0 3.5 %fusion.19 = bf16[1024,768]{1,0:T(8,128)(2,1)} fusion(bf16[1024,768]{1,0:T(8,128)(2,1)} %get-tuple-element.38, bf16[1024,768]{1,0:T(8,128)(2,1)} %gather_fusion, f32[1024]{0:T(1024)S(1)} %add_divide_fusion), kind=kLoop, calls=%fused_computation.27 | loop fusion | flops 3932160 | bytes 4722688 | tf_op jit(solution)/shard_map/convert_element_type | solution.py:92
  (23 shorter events, 0.1 us)
Async XLA Ops:
  6.5 190.6 %copy-start = (bf16[768,128]{1,0:T(8,128)(2,1)S(1)}, bf16[768,128]{1,0:T(8,128)(2,1)}, u32[]{:S(2)}) copy-start(bf16[768,128]{1,0:T(8,128)(2,1)} %param.17) | copy-start | bytes 589828
  6.5 5.2 %copy-start.1 = (bf16[2,512,768]{2,1,0:T(8,128)(2,1)S(1)}, bf16[2,512,768]{2,1,0:T(8,128)(2,1)}, u32[]{:S(2)}) copy-start(bf16[2,512,768]{2,1,0:T(8,128)(2,1)} %param.11) | copy-start | bytes 4718596
  6.5 5.2 %copy-start.3 = (f32[768]{0:T(1024)S(1)}, f32[768]{0:T(1024)}, u32[]{:S(2)}) copy-start(f32[768]{0:T(1024)} %param.15) | copy-start | bytes 9220
  6.5 55.0 %all-gather.3.cloned.1.call-start = ((), (), s32[]{:S(2)}) async-start(), calls=%async_computation.2 | async-start | bytes 3760128 | tf_op jit(solution)/shard_map/all_gather | solution.py:28
  7.3 99.2 %all-gather.5.cloned.1.call-start = ((), (), s32[]{:S(2)}) async-start(), calls=%async_computation.3 | async-start | bytes 1253376 | tf_op jit(solution)/shard_map/all_gather | solution.py:43
  106.5 4.0 %copy-start.4 = (f32[768]{0:T(1024)S(1)}, f32[768]{0:T(1024)}, u32[]{:S(2)}) copy-start(f32[768]{0:T(1024)} %param.16) | copy-start | bytes 9220
  192.3 4.8 %copy-start.2 = (s32[2,512,1]{1,2,0:T(1,128)S(1)}, s32[2,512,1]{1,2,0:T(1,128)}, u32[]{:S(2)}) copy-start(s32[2,512,1]{1,2,0:T(1,128)} %param.12) | copy-start | bytes 12292
  192.3 46.5 %all-to-all-start.1 = ((bf16[128,2,8,768]{3,2,1,0:T(8,128)(2,1)}), bf16[128,2,8,768]{3,2,1,0:T(8,128)(2,1)S(1)}, u32[]{:S(2)}, u32[]{:S(2)}) async-start(bf16[128,2,8,768]{3,2,1,0:T(8,128)(2,1)} %bitcast.100), calls=%async_computation.1 | async-start | bytes 6291456 | tf_op jit(solution)/shard_map/all_to_all | solution.py:79
Sparse Core Ops, SparseCore 0:
  9.5 51.9 all-gather.2
  63.7 40.5 all-gather.4
where the time goes:
time: 255 us; the launch traced here: 254 us
  waiting for transfers between devices  89.1 us (35%)
  matrix products  49.9 us (20%)
  blocking collectives  49.2 us (19%)
  local copies, waits for them, and re-layouts  33 us (13%)
  other arithmetic  14.9 us (6%)
  between operations  13.6 us (5%)
  starting transfers between devices  4.79 us (2%)
    all_to_all x1, blocking collectives, body(): lax.all_to_all(outgoing, ('seq', 'role', 'exp'), split_axis=0, concat_axi...  49.2 us
    all_gather x1, waiting for transfers between devices, body(): lax.all_gather(attn_qkv, ('seq', 'role'), axis=0, tiled=True)  48.2 us
    all_to_all x1, waiting for transfers between devices, body(): lax.all_to_all(jnp.dot(hidden, weight_out, preferred_element_type=jnp.flo...  39.5 us
    dot_general x1, matrix products, body(): jnp.dot(hidden, weight_out, preferred_element_type=jnp.float32)  25.4 us
    dot_general x2, matrix products, add_columns(): return jnp.dot(source, weight_piece, preferred_element_type=jnp.float32)  12.4 us
    reshape x1, local copies, waits for them, and re-layouts, body(): heads_split = projected.reshape(token_count // LEN, LEN, 3, HEADS, head_dim)  8.81 us
    scatter x1, other arithmetic, body(): jnp.zeros((slots_total, model_width), jnp.bfloat16).at[position]  7.21 us
    while x2, local copies, waits for them, and re-layouts, body(): context = lax.map(attend, heads_split).reshape(token_count, model_width)  7.17 us
  transfers between devices with their start and end apart: 3, of which 2 were waited for; matrix products, arithmetic and copies ran while one was open for 21% of the time, Pallas kernels for 0%

commit v1 on v0

--- a/solution.py
+++ b/solution.py
@@ -24,9 +24,16 @@
     head_dim = model_width // HEADS
     flat_tokens = tokens.reshape(token_count, model_width)
     normed = scale_rows(flat_tokens, norm_attn).astype(jnp.bfloat16)
-    projected = add_columns(
-        normed, lax.all_gather(attn_qkv, ("seq", "role"), axis=0, tiled=True)
-    ).astype(jnp.bfloat16)
+    _spread_words = lambda slab_in, at_axis: jnp.concatenate(
+        lax.all_to_all(
+            jnp.stack([slab_in for _ in range(lax.axis_size(("seq", "role")))]),
+            split_axis=0,
+            axis_name=("seq", "role"),
+            concat_axis=0,
+        ),
+        at_axis,
+    )
+    projected = add_columns(normed, _spread_words(attn_qkv, 0)).astype(jnp.bfloat16)
     heads_split = projected.reshape(token_count // LEN, LEN, 3, HEADS, head_dim)
 
     def attend(sequence):

time: 255 us -> 265 us (1.039)
  starting transfers between devices: 4.79 us -> 13.4 us
  blocking collectives: 49.2 us -> 56.3 us
  waiting for transfers between devices: 89.1 us -> 83.3 us
    all_gather x1 -> x0, waiting for transfers between devices: 48.2 us -> none  [body(): lax.all_gather(attn_qkv, ('seq', 'role'), axis=0, tiled=True)]
    all_to_all x0 -> x1, waiting for transfers between devices: none -> 43.1 us  [body(): lax.all_to_all(jnp.stack([slab_in for _ in range(lax.axis_size(('seq', 'r...]
    all_to_all x0 -> x1, starting transfers between devices: none -> 8.59 us  [body(): lax.all_to_all(jnp.stack([slab_in for _ in range(lax.axis_size(('seq', 'r...]
    all_to_all x1, blocking collectives: 49.2 us -> 56.3 us  [body(): lax.all_to_all(outgoing, ('seq', 'role', 'exp'), split_axis=0, concat_axi...]
    another operation x0 -> x1, local copies, waits for them, and re-layouts: none -> 2.96 us  [body(): jnp.stack([slab_in for _ in range(lax.axis_size(('seq', 'role')))])]
  transfers between devices with their start and end apart: 3 -> 3, of which waited for: 2 -> 2; matrix products, arithmetic and copies ran while one was open for 21% -> 19% of each run, Pallas kernels for 0% -> 0%
where the time goes in v1:
time: 265 us; the launch traced here: 264 us
  waiting for transfers between devices  83.3 us (31%)
  blocking collectives  56.3 us (21%)
  matrix products  49.8 us (19%)
  local copies, waits for them, and re-layouts  35.2 us (13%)
  between operations  13.6 us (5%)
  starting transfers between devices  13.4 us (5%)
  other arithmetic  12.8 us (5%)
    all_to_all x1, blocking collectives, body(): lax.all_to_all(outgoing, ('seq', 'role', 'exp'), split_axis=0, concat_axi...  56.3 us
    all_to_all x1, waiting for transfers between devices, body(): lax.all_to_all(jnp.stack([slab_in for _ in range(lax.axis_size(('seq', 'r...  43.1 us
    all_to_all x1, waiting for transfers between devices, body(): lax.all_to_all(jnp.dot(hidden, weight_out, preferred_element_type=jnp.flo...  39.5 us
    dot_general x1, matrix products, body(): jnp.dot(hidden, weight_out, preferred_element_type=jnp.float32)  25.4 us
    dot_general x2, matrix products, add_columns(): return jnp.dot(source, weight_piece, preferred_element_type=jnp.float32)  12.4 us
    reshape x1, local copies, waits for them, and re-layouts, body(): heads_split = projected.reshape(token_count // LEN, LEN, 3, HEADS, head_dim)  8.82 us
    all_to_all x1, starting transfers between devices, body(): lax.all_to_all(jnp.stack([slab_in for _ in range(lax.axis_size(('seq', 'r...  8.59 us
    scatter x1, other arithmetic, body(): jnp.zeros((slots_total, model_width), jnp.bfloat16).at[position]  7.21 us
  transfers between devices with their start and end apart: 3, of which 2 were waited for; matrix products, arithmetic and copies ran while one was open for 19% of the time, Pallas kernels for 0%

profile of v1, /device:TPU:1, one launch (start us, length us, event | category | flops | bytes accessed | tf_op | source)
XLA Modules:
  0.0 264.5 jit_solution(7236456382387600161)
XLA Ops:
  6.5 3.0 %stack.2 = bf16[16,48,2304]{2,1,0:T(8,128)(2,1)} broadcast(bf16[48,2304]{1,0:T(8,128)(2,1)} %param.13), dimensions={1,2} | broadcast | bytes 3760128 | tf_op jit(solution)/shard_map/stack | solution.py:29
  9.5 8.6 %all-to-all-start = ((bf16[16,48,2304]{2,1,0:T(8,128)(2,1)}), bf16[16,48,2304]{2,1,0:T(8,128)(2,1)}, u32[]{:S(2)}, u32[]{:S(2)}) async-start(bf16[16,48,2304]{2,1,0:T(8,128)(2,1)} %stack.2), calls=%async_computation | async-start | bytes 7077888 | tf_op jit(solution)/shard_map/all_to_all | solution.py:28
  18.1 0.0 all-gather.2.cloned.1.call-start
  18.2 0.7 all-gather.2.cloned.1.call-update
  18.9 0.4 fusion.25
  19.3 0.1 broadcast_bitcast_fusion
  19.4 0.4 multiply_reduce_fusion
  19.8 1.6 multiply_convert_fusion
  21.4 43.1 %all-to-all-done = bf16[16,48,2304]{2,1,0:T(8,128)(2,1)} async-done(((bf16[16,48,2304]{2,1,0:T(8,128)(2,1)}), bf16[16,48,2304]{2,1,0:T(8,128)(2,1)}, u32[]{:S(2)}, u32[]{:S(2)}) %all-to-all-start) | async-done | bytes 3538976 | tf_op jit(solution)/shard_map/all_to_all | solution.py:28
  64.5 8.4 %convolution_convert_fusion = bf16[1024,2304]{1,0:T(8,128)(2,1)} fusion(bf16[1024,768]{1,0:T(8,128)(2,1)} %bitcast.96, bf16[768,2304]{1,0:T(8,128)(2,1)} %bitcast.8), kind=kOutput, calls=%fused_computation.16 | convolution fusion | flops 3626237952 | bytes 9830400 | tf_op jit(solution)/shard_map/dot_general | solution.py:16
  72.9 6.7 %copy.13 = bf16[1024,2304]{0,1:T(8,128)(2,1)} copy(bf16[1024,2304]{1,0:T(8,128)(2,1)} %convolution_convert_fusion) | data formatting | bytes 9437184 | tf_op jit(solution)/shard_map/convert_element_type | solution.py:36
  79.6 8.8 %reshape.138 = bf16[2,512,3,12,64]{1,0,4,3,2:T(2,128)(2,1)} reshape(bf16[1024,2304]{0,1:T(8,128)(2,1)} %copy.13) | data formatting | bytes 9437184 | tf_op jit(solution)/shard_map/reshape | solution.py:37
  88.4 5.5 %copy.14 = bf16[2,512,3,12,64]{1,4,3,2,0:T(8,128)(2,1)} copy(bf16[2,512,3,12,64]{1,0,4,3,2:T(2,128)(2,1)} %reshape.138) | data formatting | bytes 9437184 | tf_op jit(solution)/shard_map/while | solution.py:49
  94.0 13.4 %while.10 = (s32[]{:T(128)}, bf16[2,512,12,64]{1,3,2,0:T(8,128)(2,1)S(1)}, bf16[2,512,3,12,64]{1,4,3,2,0:T(8,128)(2,1)}, s32[]{:T(128)}) while((s32[]{:T(128)}, bf16[2,512,12,64]{1,3,2,0:T(8,128)(2,1)S(1)}, bf16[2,512,3,12,64]{1,4,3,2,0:T(8,128)(2,1)}, s32[]{:T(128)}) %tuple.24), condition=%wide.region_3.4_spmd, body=%wide.region_1.3_spmd.sunk | while | flops 821422080 | bytes 33087548 | solution.py:49
  94.0 1.9 dynamic-slice_bitcast_fusion.2
  95.9 2.3 fusion.40
  98.2 2.4 fusion.41
  100.6 1.9 dynamic-slice_bitcast_fusion.2
  102.6 2.3 fusion.40
  104.9 2.4 fusion.41
  107.3 1.6 copy.15
  109.0 0.4 copy.18
  109.4 0.0 all-gather.2.cloned.1.call-done
  109.4 4.0 %fusion.16 = (f32[1024]{0:T(1024)S(1)}, bf16[1024,768]{1,0:T(8,128)(2,1)}) fusion(bf16[1024,768]{0,1:T(8,128)(2,1)S(1)} %bitcast.97, bf16[768,768]{1,0:T(8,128)(2,1)} %all-gather.2.cloned.1.call-done, bf16[2,512,768]{2,1,0:T(8,128)(2,1)S(1)} %copy-done.1), kind=kOutput, calls=%fused_computation.24 | convolution fusion | flops 1212677120 | bytes 5902336 | tf_op jit(solution)/shard_map/dot_general | solution.py:16
  113.4 7.2 %scatter_custom_fusion = bf16[2048,768]{1,0:T(8,128)(2,1)S(1)} fusion(s32[1024]{0:T(1024)S(1)} %bitcast.99, bf16[]{:T(256)} %constant.7.clone.1, bf16[1024,768]{1,0:T(8,128)(2,1)} %get-tuple-element.38, f32[768]{0:T(1024)S(1)} %copy-done.5, f32[1024]{0:T(1024)S(1)} %add_rsqrt_fusion), kind=kCustom, calls=%fused_computation.32 | custom fusion | flops 3145728 | bytes 4726786 | tf_op jit(solution)/shard_map/scatter | solution.py:75
  120.6 56.3 %all_to_all.15 = bf16[128,2,8,768]{3,2,1,0:T(8,128)(2,1)} all-to-all(bf16[128,2,8,768]{3,2,1,0:T(8,128)(2,1)S(1)} %bitcast.92), channel_id=1, replica_groups=mesh['seq'=8,'role'=2,'exp'=8] {'seq','role','exp'}, dimensions={0} | all-to-all | bytes 6291456 | tf_op jit(solution)/shard_map/all_to_all | solution.py:79
  176.9 25.4 %fusion.11 = bf16[2048,768]{1,0:T(8,128)(2,1)} fusion(bf16[1,3072,768]{2,1,0:T(8,128)(2,1)} %param.19, bf16[2048,768]{1,0:T(8,128)(2,1)} %bitcast.95, bf16[1,768,3072]{2,1,0:T(8,128)(2,1)} %param.18), kind=kOutput, calls=%fused_computation.23 | convolution fusion | flops 19341508608 | bytes 15728640 | tf_op jit(solution)/shard_map/dot_general | solution.py:87
  202.4 4.8 %all-to-all-start.2 = ((bf16[128,2,8,768]{3,2,1,0:T(8,128)(2,1)}), bf16[128,2,8,768]{3,2,1,0:T(8,128)(2,1)S(1)}, u32[]{:S(2)}, u32[]{:S(2)}) async-start(bf16[128,2,8,768]{3,2,1,0:T(8,128)(2,1)} %bitcast.94), calls=%async_computation.2 | async-start | bytes 6291456 | tf_op jit(solution)/shard_map/all_to_all | solution.py:86
  207.2 2.2 fusion.24
  209.3 39.5 %all-to-all-done.2 = bf16[128,2,8,768]{3,2,1,0:T(8,128)(2,1)S(1)} async-done(((bf16[128,2,8,768]{3,2,1,0:T(8,128)(2,1)}), bf16[128,2,8,768]{3,2,1,0:T(8,128)(2,1)S(1)}, u32[]{:S(2)}, u32[]{:S(2)}) %all-to-all-start.2) | async-done | bytes 3145760 | tf_op jit(solution)/shard_map/all_to_all | solution.py:86
  248.9 5.2 %gather_fusion = bf16[1024,768]{1,0:T(8,128)(2,1)} fusion(bf16[2048,768]{1,0:T(8,128)(2,1)S(1)} %bitcast.91, s32[1024]{0:T(1024)S(1)} %broadcast_clamp_fusion), kind=kCustom, calls=%fused_computation | custom fusion | bytes 3149824 | tf_op jit(solution)/shard_map/gather | solution.py:96
  254.1 3.5 %fusion.19 = bf16[1024,768]{1,0:T(8,128)(2,1)} fusion(bf16[1024,768]{1,0:T(8,128)(2,1)} %get-tuple-element.38, bf16[1024,768]{1,0:T(8,128)(2,1)} %gather_fusion, f32[1024]{0:T(1024)S(1)} %add_divide_fusion), kind=kLoop, calls=%fused_computation.27 | loop fusion | flops 3932160 | bytes 4722688 | tf_op jit(solution)/shard_map/convert_element_type | solution.py:99
  (24 shorter events, 0.1 us)
Async XLA Ops:
  6.5 200.6 %copy-start = (bf16[768,128]{1,0:T(8,128)(2,1)S(1)}, bf16[768,128]{1,0:T(8,128)(2,1)}, u32[]{:S(2)}) copy-start(bf16[768,128]{1,0:T(8,128)(2,1)} %param.17) | copy-start | bytes 589828
  9.5 9.4 %copy-start.2 = (s32[2,512,1]{1,2,0:T(1,128)S(1)}, s32[2,512,1]{1,2,0:T(1,128)}, u32[]{:S(2)}) copy-start(s32[2,512,1]{1,2,0:T(1,128)} %param.12) | copy-start | bytes 12292
  9.5 9.9 %copy-start.1 = (bf16[2,512,768]{2,1,0:T(8,128)(2,1)S(1)}, bf16[2,512,768]{2,1,0:T(8,128)(2,1)}, u32[]{:S(2)}) copy-start(bf16[2,512,768]{2,1,0:T(8,128)(2,1)} %param.11) | copy-start | bytes 4718596
  9.5 10.3 %copy-start.4 = (f32[768]{0:T(1024)S(1)}, f32[768]{0:T(1024)}, u32[]{:S(2)}) copy-start(f32[768]{0:T(1024)} %param.15) | copy-start | bytes 9220
  9.5 55.0 %all-to-all-start = ((bf16[16,48,2304]{2,1,0:T(8,128)(2,1)}), bf16[16,48,2304]{2,1,0:T(8,128)(2,1)}, u32[]{:S(2)}, u32[]{:S(2)}) async-start(bf16[16,48,2304]{2,1,0:T(8,128)(2,1)} %stack.2), calls=%async_computation | async-start | bytes 7077888 | tf_op jit(solution)/shard_map/all_to_all | solution.py:28
  18.1 91.3 %all-gather.2.cloned.1.call-start = ((), (), s32[]{:S(2)}) async-start(), calls=%async_computation.3 | async-start | bytes 1253376 | tf_op jit(solution)/shard_map/all_gather | solution.py:50
  109.4 4.0 %copy-start.5 = (f32[768]{0:T(1024)S(1)}, f32[768]{0:T(1024)}, u32[]{:S(2)}) copy-start(f32[768]{0:T(1024)} %param.16) | copy-start | bytes 9220
  202.4 4.8 %copy-start.3 = (s32[2,512,1]{1,2,0:T(1,128)S(1)}, s32[2,512,1]{1,2,0:T(1,128)}, u32[]{:S(2)}) copy-start(s32[2,512,1]{1,2,0:T(1,128)} %param.12) | copy-start | bytes 12292
  202.4 46.5 %all-to-all-start.2 = ((bf16[128,2,8,768]{3,2,1,0:T(8,128)(2,1)}), bf16[128,2,8,768]{3,2,1,0:T(8,128)(2,1)S(1)}, u32[]{:S(2)}, u32[]{:S(2)}) async-start(bf16[128,2,8,768]{3,2,1,0:T(8,128)(2,1)} %bitcast.94), calls=%async_computation.2 | async-start | bytes 6291456 | tf_op jit(solution)/shard_map/all_to_all | solution.py:86
Sparse Core Ops, SparseCore 0:
  21.1 67.6 all-gather.1
